TPU v7x, 512 devices: a whole 4x4x16 slice. The times are simulated.
512 devices in a mesh: pipe: 16 (over z_lo, y), dp: 32 (over z_hi, x, core).
Axes of the slice: x: 4, y: 4, z: 16 (z_hi: 4, z_lo: 4; z = z_hi * 4 + z_lo), core: 2. Of those that a mesh axis runs over, the one named last changes fastest.
Arguments:
- queries: bfloat16 [16, 4096, 4096], P('pipe', 'dp'), may hold values from -6 to 6
- out_grad: bfloat16 [16, 4096, 4096], P('pipe', 'dp'), may hold values from -6 to 6
- keys: bfloat16 [16, 2048, 512], P('pipe', 'dp'), may hold values from -6 to 6
- values: bfloat16 [16, 2048, 512], P('pipe', 'dp'), may hold values from -6 to 6
- kv_weight: bfloat16 [16, 8192, 1024], P('pipe', 'dp'), may hold values from -0.0625 to 0.0625
- stream: bfloat16 [2048, 8192], P(None, 'dp'), may hold values from -640 to 640
- norm_gain: float32 [8192], P('dp'), may hold values from 0.1 to 1.9
- lengths: int32 [32], P('dp'), may hold values from 32 to 128, as said below
Outputs:
- kv_weight_grad: float32 [16, 8192, 1024], P('pipe', 'dp')
- latent_grad: bfloat16 [2048, 8192], P('pipe', 'dp')
- gain_grad: float32 [8192], P('dp')
Inputs may be any that keep to these rules, and one draw needn't show every extreme that they name: `lengths`: each micro-batch has 32 to 128 live tokens; some micro-batch has exactly 128 and another exactly 32.
All inputs are finite; a program needn't handle non-finite values.
Results may differ from a plain program's by a relative error of at most 0.0057.
Values may be sent and summed in bfloat16 or wider, within the bound.
A program may use at most 64 MiB of HBM per device.

v0:
```python
import math

import jax
import jax.numpy as jnp
from jax import lax
from jax.sharding import PartitionSpec as P

D = 8192
HQ = 32
KVH = 4
HD = 128


NORM_EPS = 1e-05


def attention_grads(query_rows, grad_rows, key_rows, value_rows, length):
    token_count = query_rows.shape[0]
    latent_count = key_rows.shape[0]
    group_size = HQ // KVH
    score_scale = 1.0 / math.sqrt(HD)
    token_live = lax.iota(jnp.int32, token_count) < length
    masked = jnp.where(token_live[:, None], grad_rows, jnp.zeros_like(grad_rows))
    query_h = query_rows.reshape(token_count, KVH, group_size, HD)
    grad_h = masked.reshape(token_count, KVH, group_size, HD)
    key_h = key_rows.reshape(latent_count, KVH, HD)
    value_h = value_rows.reshape(latent_count, KVH, HD)
    scores = (
        jnp.einsum("tgqd,jgd->gqjt", query_h, key_h, preferred_element_type=jnp.float32)
        * score_scale
    )
    row_max = jnp.max(scores, axis=2, keepdims=True)
    expo = jnp.exp(scores - row_max)
    prob_values = expo / jnp.sum(expo, axis=2, keepdims=True)
    dprob = jnp.einsum("tgqd,jgd->gqjt", grad_h, value_h, preferred_element_type=jnp.float32)
    centre = jnp.sum(prob_values * dprob, axis=2, keepdims=True)
    dscore = (prob_values * (dprob - centre) * score_scale).astype(jnp.bfloat16)
    probs_b = prob_values.astype(jnp.bfloat16)
    key_grad = jnp.einsum("gqjt,tgqd->jgd", dscore, query_h, preferred_element_type=jnp.float32)
    value_grad = jnp.einsum("gqjt,tgqd->jgd", probs_b, grad_h, preferred_element_type=jnp.float32)
    joined = jnp.concatenate(
        [key_grad.reshape(latent_count, KVH * HD), value_grad.reshape(latent_count, KVH * HD)],
        axis=1,
    )
    return joined.astype(jnp.bfloat16)


def body(queries, out_grad, keys, values, kv_weight, stream, norm_gain, lengths):
    kv_grads = attention_grads(queries[0], out_grad[0], keys[0], values[0], lengths[0])
    promoted = stream.astype(jnp.float32)
    squares = lax.psum(jnp.sum(promoted * promoted, axis=1), "dp")
    inverse = lax.rsqrt(squares / D + NORM_EPS)[:, None]
    normed = promoted * inverse
    latents = (normed * norm_gain[None, :]).astype(jnp.bfloat16)
    gathered = lax.all_gather(kv_grads, "dp", axis=0, tiled=True)
    group_total = lax.axis_size("dp")
    weight = kv_weight[0]
    weight_grad = (
        lax.dot_general(
            latents, gathered, (((0,), (0,)), ((), ())), preferred_element_type=jnp.float32
        )
        / group_total
    )
    row_count = gathered.shape[0] // lax.axis_size("pipe")
    first_row = lax.axis_index("pipe") * row_count
    share_rows = lax.psum_scatter(
        lax.dot_general(
            gathered, weight, (((1,), (1,)), ((), ())), preferred_element_type=jnp.float32
        ),
        "pipe",
        scatter_dimension=0,
        tiled=True,
    )
    normed_share = lax.dynamic_slice_in_dim(normed, first_row, row_count, 0)
    gain_part = jnp.sum(share_rows * normed_share, axis=0)
    gain_grad = lax.psum(gain_part, "pipe") / group_total
    return (weight_grad[None], share_rows.astype(jnp.bfloat16), gain_grad)


def solution(mesh):
    return jax.shard_map(
        body,
        mesh=mesh,
        in_specs=(
            P("pipe", "dp", None),
            P("pipe", "dp", None),
            P("pipe", "dp", None),
            P("pipe", "dp", None),
            P("pipe", "dp", None),
            P(None, "dp"),
            P("dp"),
            P("dp"),
        ),
        out_specs=(P("pipe", "dp", None), P("pipe", "dp"), P("dp")),
        check_vma=False,
    )
```

profile of v0, /device:TPU:8, one launch (start us, length us, event | category | flops | bytes accessed | tf_op | source)
XLA Modules:
  0.0 271.0 jit_solution(11565212643555635086)
XLA Ops:
  7.2 0.0 copy-start
  7.2 0.0 copy-start.3
  7.2 0.0 all-gather.2.cloned.1.call-start
  7.2 1.5 copy.33
  8.7 0.0 copy-done.3
  8.8 0.0 copy-start.2
  8.8 0.5 fusion.9
  9.3 0.0 copy-start.4
  9.3 1.2 fusion.32
  10.5 0.0 copy-done.2
  10.5 1.2 copy.34
  12.4 0.0 copy-done.4
  12.4 2.8 %convolution_bitcast_fusion = f32[4,8,64,128]{3,2,1,0:T(8,128)} fusion(bf16[128,4,8,128]{3,2,1,0:T(8,128)(2,1)} %bitcast.53, pred[128]{0:T(512)(128)(4,1)S(1)} %iota_compare_fusion, bf16[64,4,128,1]{2,1,0,3:T(4,128)(2,1)S(1)} %bitcast.56), kind=kOutput, calls=%fused_computation.13 | convolution fusion | flops 67633152 | bytes 2162816 | tf_op jit(solution)/shard_map/tgqd,jgd->gqjt/dot_general | solution.py:35
  15.2 1.9 fusion.15
  17.2 2.9 %fusion.16 = bf16[4,8,8,128]{3,2,1,0:T(8,128)(2,1)S(1)} fusion(f32[4,8,64,128]{3,2,1,0:T(8,128)} %convolution_bitcast_fusion, bf16[128,4,8,128]{3,2,1,0:T(8,128)(2,1)S(1)} %bitcast.50, f32[4,8,64,128]{3,2,1,0:T(8,128)} %get-tuple-element.6, f32[4,8,128]{2,1,0:T(8,128)S(1)} %get-tuple-element.5), kind=kOutput, calls=%fused_computation.23 | convolution fusion | flops 68980800 | bytes 3227648 | tf_op jit(solution)/shard_map/gqjt,tgqd->jgd/dot_general | solution.py:39
  20.1 0.7 pad_maximum_fusion
  20.8 0.0 all-gather.2.cloned.1.call-update
  20.8 0.0 reduce-scatter.2.cloned.1.call-start
  20.9 100.0 %all-gather.2.cloned.1.call-done = bf16[2048,1024]{1,0:T(8,128)(2,1)} async-done(((bf16[64,1024]{1,0:T(8,128)(2,1)}), bf16[2048,1024]{1,0:T(8,128)(2,1)}) %all-gather.2.cloned.1.call-update) | async-done | bytes 4194320 | tf_op jit(solution)/shard_map/all_gather | solution.py:55
  120.9 0.0 copy-done
  120.9 4.8 %fusion.22 = f32[2048,256]{1,0:T(8,128)} fusion(bf16[2048,1024]{1,0:T(8,128)(2,1)} %all-gather.2.cloned.1.call-done, bf16[1,256,1024]{2,1,0:T(8,128)(2,1)S(1)} %copy-done), kind=kOutput, calls=%fused_computation.30 | convolution fusion | flops 1073741824 | bytes 6815744 | tf_op jit(solution)/shard_map/dot_general | solution.py:67
  125.7 0.0 copy-start.1
  125.7 0.0 reduce-scatter.2.cloned.1.call-update
  125.7 1.2 copy-done.1
  126.9 0.0 copy-start.5
  126.9 0.3 fusion.2
  127.2 89.8 %psum.14 = f32[2048]{0:T(1024)S(1)} all-reduce(f32[2048]{0:T(1024)S(1)} %fusion.2), channel_id=1, replica_groups=mesh['pipe'=16,'dp'=32] {'dp'}, use_global_device_ids=true, to_apply=%region_1.2 | all-reduce | flops 2048 | bytes 16384 | tf_op jit(solution)/shard_map/psum | solution.py:51
  217.0 1.7 convert_multiply_fusion
  218.7 0.0 copy-done.5
  218.7 4.5 %fusion.8 = f32[1,256,1024]{2,1,0:T(8,128)} fusion(bf16[2048,1024]{1,0:T(8,128)(2,1)} %all-gather.2.cloned.1.call-done, f32[256]{0:T(256)S(1)} %copy-done.5, bf16[2048,256]{1,0:T(8,128)(2,1)S(1)} %copy-done.1, f32[2048]{0:T(1024)S(1)} %add_rsqrt_fusion), kind=kOutput, calls=%fused_computation.12 | convolution fusion | flops 1076101120 | bytes 6300672 | tf_op jit(solution)/shard_map/dot_general | solution.py:59
  223.3 0.0 reduce-scatter.2.cloned.1.call-done
  223.3 1.7 multiply_reduce_fusion.1
  224.9 38.6 %psum.15 = f32[256]{0:T(256)S(1)} all-reduce(f32[256]{0:T(256)S(1)} %get-tuple-element.3), channel_id=1, replica_groups=mesh['pipe'=16,'dp'=32] {'pipe'}, use_global_device_ids=true, to_apply=%region_7.8 | all-reduce | flops 256 | bytes 2048 | tf_op jit(solution)/shard_map/psum | solution.py:76
  263.6 0.6 broadcast_multiply_fusion
  (5 shorter events, 0.1 us)
Async XLA Ops:
  7.2 113.7 %copy-start = (bf16[1,256,1024]{2,1,0:T(8,128)(2,1)S(1)}, bf16[1,256,1024]{2,1,0:T(8,128)(2,1)}, u32[]{:S(2)}) copy-start(bf16[1,256,1024]{2,1,0:T(8,128)(2,1)} %param.12) | copy-start | bytes 1572868
  7.2 1.6 copy-start.3
  7.2 113.7 %all-gather.2.cloned.1.call-start = ((), (), s32[]{:S(2)}) async-start(), calls=%async_computation.1 | async-start | bytes 4325376 | tf_op jit(solution)/shard_map/all_gather | solution.py:55
  8.8 1.7 copy-start.2
  9.3 3.1 %copy-start.4 = (bf16[1,64,512]{2,1,0:T(8,128)(2,1)S(1)}, bf16[1,64,512]{2,1,0:T(8,128)(2,1)}, u32[]{:S(2)}) copy-start(bf16[1,64,512]{2,1,0:T(8,128)(2,1)} %param.11) | copy-start | bytes 196612
  20.8 202.4 %reduce-scatter.2.cloned.1.call-start = ((), (), s32[]{:S(2)}) async-start(), calls=%async_computation.2 | async-start | bytes 2228224 | tf_op jit(solution)/shard_map/reduce_scatter | solution.py:66
  125.7 1.2 copy-start.1
  126.9 91.8 %copy-start.5 = (f32[256]{0:T(256)S(1)}, f32[256]{0:T(256)}, u32[]{:S(2)}) copy-start(f32[256]{0:T(256)} %param.14) | copy-start | bytes 3076
Sparse Core Ops, SparseCore 0:
  20.9 99.8 all-gather.1
  125.8 84.4 reduce-scatter.1
where the time goes:
time: 271 us
  blocking collectives  128 us (47%)
  waiting for transfers between devices  100 us (37%)
  matrix products  17.6 us (6%)
  between operations  14.8 us (5%)
  other arithmetic  6.15 us (2%)
  local copies, waits for them, and re-layouts  3.97 us (1%)
    all_gather x1, waiting for transfers between devices, body(): gathered = lax.all_gather(kv_grads, 'dp', axis=0, tiled=True)  100 us
    psum x1, blocking collectives, body(): squares = lax.psum(jnp.sum(promoted * promoted, axis=1), 'dp')  89.8 us
    psum x1, blocking collectives, body(): gain_grad = lax.psum(gain_part, 'pipe') / group_total  38.6 us
  transfers between devices with their start and end apart: 2, of which 1 were waited for; matrix products, arithmetic and copies ran while one was open for 2% of the time, Pallas kernels for 0%

commit v1 on v0

--- a/solution.py
+++ b/solution.py
@@ -3,6 +3,8 @@
 import jax
 import jax.numpy as jnp
 from jax import lax
+from jax.experimental import pallas as pl
+from jax.experimental.pallas import tpu as pltpu
 from jax.sharding import PartitionSpec as P
 
 D = 8192
@@ -45,36 +47,298 @@
     return joined.astype(jnp.bfloat16)
 
 
+ROWS = 2048
+COLS = 256
+KVC = 1024
+LAT = 64
+HALF = 32
+PIPE = 16
+GROUPS = 32
+SHARE = 128
+
+GATHER = ["Zp0", "Zm1", "Zp1", "Zm0", "Fp0", "Fm1"]
+GATHER += [n + str(i) for i in range(4) for n in ("Xp0", "Xm1", "Xp1", "Xm0", "Gp0", "Gm1")]
+GATHER += ["C%d%d" % (i, j) for i in range(4) for j in range(4)]
+OTHERS = ["Qz1", "Qz2", "Qz3", "Qx1", "Qx2", "Qx3", "Qc"]
+OTHERS += [n + str(i) for i in range(4) for n in ("Yo", "Yn", "Yr")]
+OTHERS += ["L1", "L2", "L3", "Gy1", "Gy2", "Gy3", "Gl1", "Gl2", "Gl3"]
+SLOT = {n: i for i, n in enumerate(GATHER + OTHERS)}
+
+
+def exchange_kernel(
+    kv_ref, w_ref, st_ref, gn_ref, wg_ref, lat_ref, gain_ref,
+    g, xt, latt, sq, sqz, sqx, sqc, sqs, inv, tf, tb, ro, rp, rm, sr, sl, rl, gs, gy, gs2, gl,
+    send_sem, recv_sem,
+):
+    p = lax.axis_index("pipe")
+    q = lax.axis_index("dp")
+    zl, y = lax.div(p, 4), lax.rem(p, 4)
+    zh, x, c = lax.div(q, 8), lax.rem(lax.div(q, 2), 4), lax.rem(q, 2)
+
+    def up(a, k):
+        return lax.rem(a + k + 4, 4)
+
+    def dp_dev(zz, xx, cc):
+        return (p, zz * 8 + xx * 2 + cc)
+
+    def pipe_dev(zz, yy):
+        return (zz * 4 + yy, q)
+
+    z_dev = {k: dp_dev(up(zh, k), x, c) for k in (1, 2, 3)}
+    x_dev = {k: dp_dev(zh, up(x, k), c) for k in (1, 2, 3)}
+    c_dev = dp_dev(zh, x, 1 - c)
+    y_dev = {k: pipe_dev(zl, up(y, k)) for k in (1, 2, 3)}
+    l_dev = {k: pipe_dev(up(zl, k), y) for k in (1, 2, 3)}
+    peers = [*z_dev.values(), *x_dev.values(), c_dev, *y_dev.values(), *l_dev.values()]
+
+    barrier = pltpu.get_barrier_semaphore()
+    for peer in peers:
+        pl.semaphore_signal(barrier, inc=1, device_id=peer, device_id_type=pl.DeviceIdType.MESH)
+
+    started = []
+
+    def copy(name, src, dst, dev):
+        s = SLOT[name]
+        return pltpu.make_async_remote_copy(
+            src_ref=src, dst_ref=dst, send_sem=send_sem.at[s], recv_sem=recv_sem.at[s],
+            device_id=dev, device_id_type=pl.DeviceIdType.MESH,
+        )
+
+    def send(name, src, dst, dev):
+        made = copy(name, src, dst, dev)
+        made.start()
+        started.append(made)
+
+    def arrive(name, dst):
+        copy(name, dst, dst, c_dev).wait_recv()
+
+    def rows_of(zz, xx, cc, half):
+        start = ((zz * 4 + xx) * 2 + cc) * LAT
+        if half is None:
+            return pl.ds(pl.multiple_of(start, LAT), LAT)
+        return pl.ds(pl.multiple_of(start + half * HALF, HALF), HALF)
+
+    zs = [zh, up(zh, -1), up(zh, 1), up(zh, 2)]
+    xs = [x, up(x, -1), up(x, 1), up(x, 2)]
+
+    def block(zi, xi, half):
+        return g.at[rows_of(zs[zi], xs[xi], c, half)]
+
+    def own(half):
+        return kv_ref.at[pl.ds(half * HALF, HALF)]
+
+    def squares(i, carry):
+        rows = pl.ds(pl.multiple_of(i * 128, 128), 128)
+        turned = st_ref[rows, :].astype(jnp.float32).T
+        xt[:, rows] = turned.astype(jnp.bfloat16)
+        sq[pl.ds(i, 1), :] = jnp.sum(turned * turned, axis=0, keepdims=True)
+        return carry
+
+    lax.fori_loop(0, ROWS // 128, squares, 0)
+    pl.semaphore_wait(barrier, len(peers))
+
+    for name, half, dev in (("Zp0", 0, 1), ("Zm1", 1, 3), ("Zp1", 1, 1), ("Zm0", 0, 3)):
+        send(name, own(half), block(0, 0, half), z_dev[dev])
+    for k in (1, 2, 3):
+        send("Qz%d" % k, sq, sqz.at[k - 1], z_dev[k])
+    for name, half, dev in (("Xp00", 0, 1), ("Xm10", 1, 3), ("Xp10", 1, 1), ("Xm00", 0, 3)):
+        send(name, own(half), block(0, 0, half), x_dev[dev])
+    send("C00", kv_ref, block(0, 0, None), c_dev)
+    g[rows_of(zh, x, c, None), :] = kv_ref[...]
+
+    def x_send(zi, half):
+        b = block(zi, 0, half)
+        send("Xp%d%d" % (half, zi), b, b, x_dev[1])
+        send("Xm%d%d" % (half, zi), b, b, x_dev[3])
+
+    def core_send(zi, xi):
+        b = block(zi, xi, None)
+        send("C%d%d" % (zi, xi), b, b, c_dev)
+
+    def x_near(zi):
+        arrive("Xp0%d" % zi, block(zi, 1, 0))
+        send("Gp0%d" % zi, block(zi, 1, 0), block(zi, 1, 0), x_dev[1])
+        arrive("Xm1%d" % zi, block(zi, 2, 1))
+        send("Gm1%d" % zi, block(zi, 2, 1), block(zi, 2, 1), x_dev[3])
+        arrive("Xp1%d" % zi, block(zi, 1, 1))
+        core_send(zi, 1)
+        arrive("Xm0%d" % zi, block(zi, 2, 0))
+        core_send(zi, 2)
+
+    def x_far(zi):
+        arrive("Gp0%d" % zi, block(zi, 3, 0))
+        arrive("Gm1%d" % zi, block(zi, 3, 1))
+        core_send(zi, 3)
+
+    x_near(0)
+    x_far(0)
+    arrive("Zp0", block(1, 0, 0))
+    send("Fp0", block(1, 0, 0), block(1, 0, 0), z_dev[1])
+    x_send(1, 0)
+    arrive("Zm1", block(2, 0, 1))
+    send("Fm1", block(2, 0, 1), block(2, 0, 1), z_dev[3])
+    x_send(2, 1)
+    arrive("Zp1", block(1, 0, 1))
+    x_send(1, 1)
+    core_send(1, 0)
+    arrive("Zm0", block(2, 0, 0))
+    x_send(2, 0)
+    core_send(2, 0)
+    for k in (1, 2, 3):
+        arrive("Qz%d" % k, sqz.at[k - 1])
+    sqs[0] = sq[...] + sqz[0] + sqz[1] + sqz[2]
+    for k in (1, 2, 3):
+        send("Qx%d" % k, sqs.at[0], sqx.at[k - 1], x_dev[k])
+    x_near(1)
+    x_near(2)
+    for k in (1, 2, 3):
+        arrive("Qx%d" % k, sqx.at[k - 1])
+    sqs[1] = sqs[0] + sqx[0] + sqx[1] + sqx[2]
+    send("Qc", sqs.at[1], sqc, c_dev)
+    arrive("Fp0", block(3, 0, 0))
+    x_send(3, 0)
+    arrive("Fm1", block(3, 0, 1))
+    x_send(3, 1)
+    core_send(3, 0)
+    x_far(1)
+    x_far(2)
+    arrive("Qc", sqc)
+    inv[...] = lax.rsqrt((sqs[1] + sqc[...]) / D + NORM_EPS)
+
+    def normalise(i, carry):
+        rows = pl.ds(pl.multiple_of(i * 128, 128), 128)
+        normed = xt[:, rows].astype(jnp.float32) * inv[pl.ds(i, 1), :]
+        latt[:, rows] = (normed * gn_ref[...]).astype(jnp.bfloat16)
+        return carry
+
+    lax.fori_loop(0, ROWS // 128, normalise, 0)
+    x_near(3)
+    x_far(3)
+    for zi in range(4):
+        for xi in range(4):
+            arrive("C%d%d" % (zi, xi), g.at[rows_of(zs[zi], xs[xi], 1 - c, None)])
+
+    def piece(level, yy):
+        return pl.ds(pl.multiple_of((level * 4 + yy) * SHARE, SHARE), SHARE)
+
+    def level_rows(level):
+        return pl.ds(level * SHARE, SHARE)
+
+    yo, yp, ym = up(y, 2), up(y, 1), up(y, -1)
+    for level in (0, 2, 1, 3):
+        rows = pl.ds(level * 512, 512)
+        terms = lax.dot_general(
+            g[rows, :], w_ref[...], (((1,), (1,)), ((), ())), preferred_element_type=jnp.float32
+        )
+        tf[rows, :] = terms
+        tb[rows, :] = terms.astype(jnp.bfloat16)
+        low = level < 2
+        there = y_dev[1] if low else y_dev[3]
+        back = y_dev[3] if low else y_dev[1]
+        send("Yo%d" % level, tb.at[piece(level, yo)], ro.at[level_rows(level)], there)
+        into = rm if low else rp
+        send("Yn%d" % level, tb.at[piece(level, ym if low else yp)], into.at[level_rows(level)], back)
+    for level in (0, 2, 1, 3):
+        low = level < 2
+        arrive("Yo%d" % level, ro.at[level_rows(level)])
+        mine = tf[piece(level, yp if low else ym), :]
+        relayed = mine + ro[level_rows(level), :].astype(jnp.float32)
+        sr[level_rows(level), :] = relayed.astype(jnp.bfloat16)
+        into = rp if low else rm
+        send("Yr%d" % level, sr.at[level_rows(level)], into.at[level_rows(level)], y_dev[1] if low else y_dev[3])
+
+    def weight_tile(i, carry):
+        cols = pl.ds(pl.multiple_of(i * 256, 256), 256)
+        wg_ref[:, cols] = jnp.dot(latt[...], g[:, cols], preferred_element_type=jnp.float32) / GROUPS
+        return carry
+
+    lax.fori_loop(0, KVC // 256, weight_tile, 0)
+
+    for level in range(4):
+        arrive("Yn%d" % level, (rm if level < 2 else rp).at[level_rows(level)])
+        arrive("Yr%d" % level, (rp if level < 2 else rm).at[level_rows(level)])
+
+    def reduced(level):
+        part = pl.ds(pl.multiple_of(level * SHARE, SHARE), SHARE)
+        return tf[piece(level, y), :] + rp[part, :].astype(jnp.float32) + rm[part, :].astype(jnp.float32)
+
+    for k in (3, 2, 1):
+        sl[k - 1] = reduced(up(zl, k)).astype(jnp.bfloat16)
+        send("L%d" % k, sl.at[k - 1], rl.at[k - 1], l_dev[k])
+    share = reduced(zl)
+    own_inverse = jnp.broadcast_to(inv[pl.ds(p, 1), :], (128, 128)).T
+    own_stream = st_ref[pl.ds(pl.multiple_of(p * SHARE, SHARE), SHARE), :].astype(jnp.float32)
+    normed = own_stream * jnp.concatenate([own_inverse, own_inverse], axis=1)
+    for k in (1, 2, 3):
+        arrive("L%d" % k, rl.at[k - 1])
+        share = share + rl[k - 1].astype(jnp.float32)
+    lat_ref[...] = share.astype(jnp.bfloat16)
+    part = jnp.sum(share * normed, axis=0, keepdims=True)
+    gs[...] = jnp.broadcast_to(part, (8, COLS))
+    for k in (1, 2, 3):
+        send("Gy%d" % k, gs, gy.at[k - 1], y_dev[k])
+    for k in (1, 2, 3):
+        arrive("Gy%d" % k, gy.at[k - 1])
+    gs2[...] = gs[...] + gy[0] + gy[1] + gy[2]
+    for k in (1, 2, 3):
+        send("Gl%d" % k, gs2, gl.at[k - 1], l_dev[k])
+    for k in (1, 2, 3):
+        arrive("Gl%d" % k, gl.at[k - 1])
+    gain_ref[...] = (gs2[...] + gl[0] + gl[1] + gl[2]) / GROUPS
+    for made in started:
+        made.wait_send()
+
+
+def exchange(kv_grads, weight, stream, gain):
+    f32, bf16 = jnp.float32, jnp.bfloat16
+    vmem = pl.BlockSpec(memory_space=pltpu.VMEM)
+    count = len(SLOT)
+    return pl.pallas_call(
+        exchange_kernel,
+        out_shape=(
+            jax.ShapeDtypeStruct((COLS, KVC), f32),
+            jax.ShapeDtypeStruct((SHARE, COLS), bf16),
+            jax.ShapeDtypeStruct((8, COLS), f32),
+        ),
+        in_specs=[vmem] * 4,
+        out_specs=(vmem,) * 3,
+        scratch_shapes=[
+            pltpu.VMEM((ROWS, KVC), bf16),
+            pltpu.VMEM((COLS, ROWS), bf16),
+            pltpu.VMEM((COLS, ROWS), bf16),
+            pltpu.VMEM((16, 128), f32),
+            pltpu.VMEM((3, 16, 128), f32),
+            pltpu.VMEM((3, 16, 128), f32),
+            pltpu.VMEM((16, 128), f32),
+            pltpu.VMEM((2, 16, 128), f32),
+            pltpu.VMEM((16, 128), f32),
+            pltpu.VMEM((ROWS, COLS), f32),
+            pltpu.VMEM((ROWS, COLS), bf16),
+            pltpu.VMEM((512, COLS), bf16),
+            pltpu.VMEM((512, COLS), bf16),
+            pltpu.VMEM((512, COLS), bf16),
+            pltpu.VMEM((512, COLS), bf16),
+            pltpu.VMEM((3, SHARE, COLS), bf16),
+            pltpu.VMEM((3, SHARE, COLS), bf16),
+            pltpu.VMEM((8, COLS), f32),
+            pltpu.VMEM((3, 8, COLS), f32),
+            pltpu.VMEM((8, COLS), f32),
+            pltpu.VMEM((3, 8, COLS), f32),
+            pltpu.SemaphoreType.DMA((count,)),
+            pltpu.SemaphoreType.DMA((count,)),
+        ],
+        compiler_params=pltpu.CompilerParams(
+            collective_id=0, has_side_effects=True, vmem_limit_bytes=48 * 1024 * 1024
+        ),
+        name="exchange",
+    )(kv_grads, weight, stream, gain)
+
+
 def body(queries, out_grad, keys, values, kv_weight, stream, norm_gain, lengths):
     kv_grads = attention_grads(queries[0], out_grad[0], keys[0], values[0], lengths[0])
-    promoted = stream.astype(jnp.float32)
-    squares = lax.psum(jnp.sum(promoted * promoted, axis=1), "dp")
-    inverse = lax.rsqrt(squares / D + NORM_EPS)[:, None]
-    normed = promoted * inverse
-    latents = (normed * norm_gain[None, :]).astype(jnp.bfloat16)
-    gathered = lax.all_gather(kv_grads, "dp", axis=0, tiled=True)
-    group_total = lax.axis_size("dp")
-    weight = kv_weight[0]
-    weight_grad = (
-        lax.dot_general(
-            latents, gathered, (((0,), (0,)), ((), ())), preferred_element_type=jnp.float32
-        )
-        / group_total
-    )
-    row_count = gathered.shape[0] // lax.axis_size("pipe")
-    first_row = lax.axis_index("pipe") * row_count
-    share_rows = lax.psum_scatter(
-        lax.dot_general(
-            gathered, weight, (((1,), (1,)), ((), ())), preferred_element_type=jnp.float32
-        ),
-        "pipe",
-        scatter_dimension=0,
-        tiled=True,
-    )
-    normed_share = lax.dynamic_slice_in_dim(normed, first_row, row_count, 0)
-    gain_part = jnp.sum(share_rows * normed_share, axis=0)
-    gain_grad = lax.psum(gain_part, "pipe") / group_total
-    return (weight_grad[None], share_rows.astype(jnp.bfloat16), gain_grad)
+    gain = jnp.broadcast_to(norm_gain[:, None], (COLS, 128))
+    weight_grad, latent_grad, gain_grad = exchange(kv_grads, kv_weight[0], stream, gain)
+    return (weight_grad[None], latent_grad, gain_grad[0])
 
 
 def solution(mesh):

time: 271 us -> 88 us (0.32)
  the two profiles are of different devices: /device:TPU:8 before, /device:TPU:64 now
where the time goes in v1:
time: 88 us; the launch traced here: 87.4 us
  Pallas kernels  74.9 us (85%)
  local copies, waits for them, and re-layouts  5.73 us (7%)
  matrix products  4.16 us (5%)
  between operations  1.42 us (2%)
  other arithmetic  1.2 us (1%)
    pallas_call x1, Pallas kernels, exchange(): pl.pallas_call(exchange_kernel, out_shape=(jax.ShapeDtypeStruct((COLS, KV...  74.9 us
    unnamed x16, local copies, waits for them, and re-layouts  5.02 us
    dot_general x1, matrix products, attention_grads(): jnp.einsum('gqjt,tgqd->jgd', dscore, query_h, preferred_element_type=jnp....  2.38 us

profile of v1, /device:TPU:64, one launch (start us, length us, event | category | flops | bytes accessed | tf_op | source)
XLA Modules:
  0.0 87.4 jit_solution(15088273006613288897)
XLA Ops:
  0.6 0.0 copy-start.2
  0.6 1.5 %copy.29 = bf16[16,8,32,128]{3,2,1,0:T(8,128)(2,1)S(1)} copy(bf16[16,8,32,128]{3,1,2,0:T(8,128)(2,1)} %bitcast.49) | data formatting | bytes 2097152
  2.8 0.0 copy-done.2
  2.9 0.0 copy-start.3
  2.9 0.2 copy.28
  3.1 0.6 copy-done.3
  3.7 0.5 fusion.7
  4.2 1.2 %fusion.27 = (f32[4,8,128]{2,1,0:T(8,128)S(1)}, f32[4,8,64,128]{3,2,1,0:T(8,128)}) fusion(f32[4,8,64,128]{3,2,1,0:T(8,128)S(1)} %fusion.7), kind=kOutput, calls=%fused_computation.36 | output fusion | flops 524351 | bytes 2113536 | tf_op jit(solution)/shard_map/sub | solution.py:35
  5.4 0.0 copy-start.4
  5.4 0.7 fusion.13
  6.1 0.1 copy-done.4
  6.3 0.6 convolution_bitcast_fusion
  6.9 0.0 copy-start
  6.9 2.4 %fusion.14 = bf16[4,8,8,128]{3,2,1,0:T(8,128)(2,1)S(1)} fusion(f32[4,8,64,128]{3,2,1,0:T(8,128)S(1)} %convolution_bitcast_fusion, bf16[128,4,8,128]{3,2,1,0:T(8,128)(2,1)S(1)} %bitcast.48, f32[4,8,64,128]{3,2,1,0:T(8,128)} %get-tuple-element.10, f32[4,8,128]{2,1,0:T(8,128)S(1)} %get-tuple-element.9), kind=kOutput, calls=%fused_computation.17 | convolution fusion | flops 68980800 | bytes 3227648 | tf_op jit(solution)/shard_map/gqjt,tgqd->jgd/dot_general | solution.py:41
  9.3 0.0 copy-start.1
  9.3 0.0 copy-start.5
  9.3 0.7 copy-done.5
  10.0 0.1 broadcast_in_dim.26.gn_ref
  10.1 0.0 copy-done
  10.1 0.2 copy-done.1
  10.3 74.9 %exchange.1 = (f32[256,1024]{1,0:T(8,128)S(1)}, bf16[128,256]{1,0:T(8,128)(2,1)S(1)}, f32[8,256]{1,0:T(8,128)S(1)}) custom-call(bf16[64,1024]{1,0:T(8,128)(2,1)S(1)} %pad_maximum_fusion.kv_ref, bf16[256,1024]{1,0:T(8,128)(2,1)S(1)} %bitcast.46, bf16[2048,256]{1,0:T(8,128)(2,1)S(1)} %copy-done, f32[256,128]{1,0:T(8,128)S(1)} %broadcast_in_dim.26.gn_ref), custom_call_target="tpu_custom_call" | custom-call | tf_op jit(solution)/shard_map/exchange/pallas_call | solution.py:296
  85.2 0.6 slice.3
  85.8 1.0 %copy.46 = f32[1,256,1024]{2,1,0:T(8,128)} copy(f32[1,256,1024]{2,1,0:T(8,128)S(1)} %bitcast.45) | data formatting | bytes 2097152
  86.8 0.6 copy.47
  (5 shorter events, 0.1 us)
Async XLA Ops:
  0.6 2.2 %copy-start.2 = (bf16[1,128,4096]{2,1,0:T(8,128)(2,1)S(1)}, bf16[1,128,4096]{2,1,0:T(8,128)(2,1)}, u32[]{:S(2)}) copy-start(bf16[1,128,4096]{2,1,0:T(8,128)(2,1)} %param.8) | copy-start | bytes 3145732
  2.9 0.8 copy-start.3
  5.4 0.8 copy-start.4
  6.9 3.3 %copy-start = (bf16[2048,256]{1,0:T(8,128)(2,1)S(1)}, bf16[2048,256]{1,0:T(8,128)(2,1)}, u32[]{:S(2)}) copy-start(bf16[2048,256]{1,0:T(8,128)(2,1)} %st_ref.1) | copy-start | bytes 3145732
  9.3 1.1 %copy-start.1 = (bf16[1,256,1024]{2,1,0:T(8,128)(2,1)S(1)}, bf16[1,256,1024]{2,1,0:T(8,128)(2,1)}, u32[]{:S(2)}) copy-start(bf16[1,256,1024]{2,1,0:T(8,128)(2,1)} %param.12) | copy-start | bytes 1572868
  9.3 0.7 copy-start.5

commit v2 on v1

--- a/solution.py
+++ b/solution.py
@@ -60,14 +60,14 @@
 GATHER += [n + str(i) for i in range(4) for n in ("Xp0", "Xm1", "Xp1", "Xm0", "Gp0", "Gm1")]
 GATHER += ["C%d%d" % (i, j) for i in range(4) for j in range(4)]
 OTHERS = ["Qz1", "Qz2", "Qz3", "Qx1", "Qx2", "Qx3", "Qc"]
-OTHERS += [n + str(i) for i in range(4) for n in ("Yo", "Yn", "Yr")]
+OTHERS += [n + str(h) + str(i) for i in range(4) for h in range(2) for n in ("Yo", "Yn", "Yr")]
 OTHERS += ["L1", "L2", "L3", "Gy1", "Gy2", "Gy3", "Gl1", "Gl2", "Gl3"]
 SLOT = {n: i for i, n in enumerate(GATHER + OTHERS)}
 
 
 def exchange_kernel(
     kv_ref, w_ref, st_ref, gn_ref, wg_ref, lat_ref, gain_ref,
-    g, xt, latt, sq, sqz, sqx, sqc, sqs, inv, tf, tb, ro, rp, rm, sr, sl, rl, gs, gy, gs2, gl,
+    g, xt, latt, sq, sqz, sqx, sqc, sqs, inv, tf, tb, ro, rp, rm, sr, sl, rl, gs, gy, gs2, gl, share_ref,
     send_sem, recv_sem,
 ):
     p = lax.axis_index("pipe")
@@ -134,17 +134,17 @@
         sq[pl.ds(i, 1), :] = jnp.sum(turned * turned, axis=0, keepdims=True)
         return carry
 
-    lax.fori_loop(0, ROWS // 128, squares, 0)
     pl.semaphore_wait(barrier, len(peers))
 
     for name, half, dev in (("Zp0", 0, 1), ("Zm1", 1, 3), ("Zp1", 1, 1), ("Zm0", 0, 3)):
         send(name, own(half), block(0, 0, half), z_dev[dev])
-    for k in (1, 2, 3):
-        send("Qz%d" % k, sq, sqz.at[k - 1], z_dev[k])
     for name, half, dev in (("Xp00", 0, 1), ("Xm10", 1, 3), ("Xp10", 1, 1), ("Xm00", 0, 3)):
         send(name, own(half), block(0, 0, half), x_dev[dev])
     send("C00", kv_ref, block(0, 0, None), c_dev)
     g[rows_of(zh, x, c, None), :] = kv_ref[...]
+    lax.fori_loop(0, ROWS // 128, squares, 0)
+    for k in (1, 2, 3):
+        send("Qz%d" % k, sq, sqz.at[k - 1], z_dev[k])
 
     def x_send(zi, half):
         b = block(zi, 0, half)
@@ -170,8 +170,101 @@
         arrive("Gm1%d" % zi, block(zi, 3, 1))
         core_send(zi, 3)
 
+    yo, yp, ym = up(y, 2), up(y, 1), up(y, -1)
+
+    def level_rows(zi, base=0, size=512):
+        return pl.ds(pl.multiple_of(zs[zi] * 512 + base, size), size)
+
+    def part(zi, yy, half):
+        return pl.ds(pl.multiple_of(zi * 512 + yy * SHARE + half * LAT, LAT), LAT)
+
+    def slot(zi, half):
+        return pl.ds(zi * SHARE + half * LAT, LAT)
+
+    def terms(zi):
+        for xi in range(4):
+            arrive("C%d%d" % (zi, xi), g.at[rows_of(zs[zi], xs[xi], 1 - c, None)])
+        made = lax.dot_general(
+            g[level_rows(zi), :], w_ref[...], (((1,), (1,)), ((), ())), preferred_element_type=jnp.float32
+        )
+        rows = pl.ds(zi * 512, 512)
+        tf[rows, :] = made
+        tb[rows, :] = made.astype(jnp.bfloat16)
+        send("Yo0%d" % zi, tb.at[part(zi, yo, 0)], ro.at[slot(zi, 0)], y_dev[1])
+        send("Yo1%d" % zi, tb.at[part(zi, yo, 1)], ro.at[slot(zi, 1)], y_dev[3])
+        send("Yn0%d" % zi, tb.at[part(zi, ym, 0)], rm.at[slot(zi, 0)], y_dev[3])
+        send("Yn1%d" % zi, tb.at[part(zi, yp, 1)], rp.at[slot(zi, 1)], y_dev[1])
+
+    def relay(zi):
+        for half, to, into, dev in ((0, yp, rp, 1), (1, ym, rm, 3)):
+            arrive("Yo%d%d" % (half, zi), ro.at[slot(zi, half)])
+            total = tf[part(zi, to, half), :] + ro[slot(zi, half), :].astype(jnp.float32)
+            sr[slot(zi, half), :] = total.astype(jnp.bfloat16)
+            send("Yr%d%d" % (half, zi), sr.at[slot(zi, half)], into.at[slot(zi, half)], y_dev[dev])
+
+    level_sends = []
+
+    def settle(zi):
+        for half, near, far in ((0, rm, rp), (1, rp, rm)):
+            arrive("Yn%d%d" % (half, zi), near.at[slot(zi, half)])
+            arrive("Yr%d%d" % (half, zi), far.at[slot(zi, half)])
+        mine = pl.ds(pl.multiple_of(zi * 512 + y * SHARE, SHARE), SHARE)
+        got = pl.ds(zi * SHARE, SHARE)
+        total = tf[mine, :] + rp[got, :].astype(jnp.float32) + rm[got, :].astype(jnp.float32)
+        k = up(zs[zi] - zl, 0)
+
+        @pl.when(k == 0)
+        def _():
+            share_ref[...] = total
+
+        made = pltpu.make_async_remote_copy(
+            src_ref=sl.at[zi], dst_ref=rl.at[lax.max(k, 1) - 1],
+            send_sem=send_sem.at[SLOT["L1"] + lax.max(k, 1) - 1],
+            recv_sem=recv_sem.at[SLOT["L1"] + lax.max(k, 1) - 1],
+            device_id=pipe_dev(zs[zi], y), device_id_type=pl.DeviceIdType.MESH,
+        )
+
+        @pl.when(k != 0)
+        def _():
+            sl[zi] = total.astype(jnp.bfloat16)
+            made.start()
+
+        level_sends.append((k, made))
+
+    def weight_part(zi):
+        def tile(i, carry):
+            cols = pl.ds(pl.multiple_of(i * 256, 256), 256)
+            made = jnp.dot(
+                latt[:, level_rows(zi)], g[level_rows(zi), cols], preferred_element_type=jnp.float32
+            )
+            if zi == 0:
+                wg_ref[:, cols] = made
+            elif zi < 3:
+                wg_ref[:, cols] = wg_ref[:, cols] + made
+            else:
+                wg_ref[:, cols] = (wg_ref[:, cols] + made) / GROUPS
+            return carry
+
+        lax.fori_loop(0, KVC // 256, tile, 0)
+
+    def gain_part(zi, total):
+        for j in range(4):
+            rows = pl.ds(pl.multiple_of(zs[zi] * 512 + j * 128, 128), 128)
+            scale = jnp.broadcast_to(inv[pl.ds(zs[zi] * 4 + j, 1), :], (128, 128)).T
+            normed = st_ref[rows, :].astype(jnp.float32) * jnp.concatenate([scale, scale], axis=1)
+            total = total + jnp.sum(tf[pl.ds(zi * 512 + j * 128, 128), :] * normed, axis=0, keepdims=True)
+        return total
+
+    def normalise(i, carry):
+        rows = pl.ds(pl.multiple_of(i * 128, 128), 128)
+        normed = xt[:, rows].astype(jnp.float32) * inv[pl.ds(i, 1), :]
+        latt[:, rows] = (normed * gn_ref[...]).astype(jnp.bfloat16)
+        return carry
+
     x_near(0)
     x_far(0)
+    terms(0)
+    relay(0)
     arrive("Zp0", block(1, 0, 0))
     send("Fp0", block(1, 0, 0), block(1, 0, 0), z_dev[1])
     x_send(1, 0)
@@ -189,6 +282,7 @@
     sqs[0] = sq[...] + sqz[0] + sqz[1] + sqz[2]
     for k in (1, 2, 3):
         send("Qx%d" % k, sqs.at[0], sqx.at[k - 1], x_dev[k])
+    settle(0)
     x_near(1)
     x_near(2)
     for k in (1, 2, 3):
@@ -202,89 +296,47 @@
     core_send(3, 0)
     x_far(1)
     x_far(2)
+    terms(1)
+    terms(2)
     arrive("Qc", sqc)
     inv[...] = lax.rsqrt((sqs[1] + sqc[...]) / D + NORM_EPS)
-
-    def normalise(i, carry):
-        rows = pl.ds(pl.multiple_of(i * 128, 128), 128)
-        normed = xt[:, rows].astype(jnp.float32) * inv[pl.ds(i, 1), :]
-        latt[:, rows] = (normed * gn_ref[...]).astype(jnp.bfloat16)
-        return carry
-
+    x_near(3)
+    relay(1)
+    relay(2)
     lax.fori_loop(0, ROWS // 128, normalise, 0)
-    x_near(3)
     x_far(3)
+    settle(1)
+    settle(2)
+    terms(3)
+    part_sum = jnp.zeros((1, COLS), jnp.float32)
     for zi in range(4):
-        for xi in range(4):
-            arrive("C%d%d" % (zi, xi), g.at[rows_of(zs[zi], xs[xi], 1 - c, None)])
-
-    def piece(level, yy):
-        return pl.ds(pl.multiple_of((level * 4 + yy) * SHARE, SHARE), SHARE)
-
-    def level_rows(level):
-        return pl.ds(level * SHARE, SHARE)
-
-    yo, yp, ym = up(y, 2), up(y, 1), up(y, -1)
-    for level in (0, 2, 1, 3):
-        rows = pl.ds(level * 512, 512)
-        terms = lax.dot_general(
-            g[rows, :], w_ref[...], (((1,), (1,)), ((), ())), preferred_element_type=jnp.float32
-        )
-        tf[rows, :] = terms
-        tb[rows, :] = terms.astype(jnp.bfloat16)
-        low = level < 2
-        there = y_dev[1] if low else y_dev[3]
-        back = y_dev[3] if low else y_dev[1]
-        send("Yo%d" % level, tb.at[piece(level, yo)], ro.at[level_rows(level)], there)
-        into = rm if low else rp
-        send("Yn%d" % level, tb.at[piece(level, ym if low else yp)], into.at[level_rows(level)], back)
-    for level in (0, 2, 1, 3):
-        low = level < 2
-        arrive("Yo%d" % level, ro.at[level_rows(level)])
-        mine = tf[piece(level, yp if low else ym), :]
-        relayed = mine + ro[level_rows(level), :].astype(jnp.float32)
-        sr[level_rows(level), :] = relayed.astype(jnp.bfloat16)
-        into = rp if low else rm
-        send("Yr%d" % level, sr.at[level_rows(level)], into.at[level_rows(level)], y_dev[1] if low else y_dev[3])
-
-    def weight_tile(i, carry):
-        cols = pl.ds(pl.multiple_of(i * 256, 256), 256)
-        wg_ref[:, cols] = jnp.dot(latt[...], g[:, cols], preferred_element_type=jnp.float32) / GROUPS
-        return carry
-
-    lax.fori_loop(0, KVC // 256, weight_tile, 0)
-
-    for level in range(4):
-        arrive("Yn%d" % level, (rm if level < 2 else rp).at[level_rows(level)])
-        arrive("Yr%d" % level, (rp if level < 2 else rm).at[level_rows(level)])
-
-    def reduced(level):
-        part = pl.ds(pl.multiple_of(level * SHARE, SHARE), SHARE)
-        return tf[piece(level, y), :] + rp[part, :].astype(jnp.float32) + rm[part, :].astype(jnp.float32)
-
-    for k in (3, 2, 1):
-        sl[k - 1] = reduced(up(zl, k)).astype(jnp.bfloat16)
-        send("L%d" % k, sl.at[k - 1], rl.at[k - 1], l_dev[k])
-    share = reduced(zl)
-    own_inverse = jnp.broadcast_to(inv[pl.ds(p, 1), :], (128, 128)).T
-    own_stream = st_ref[pl.ds(pl.multiple_of(p * SHARE, SHARE), SHARE), :].astype(jnp.float32)
-    normed = own_stream * jnp.concatenate([own_inverse, own_inverse], axis=1)
+        part_sum = gain_part(zi, part_sum)
+    gs[...] = jnp.broadcast_to(part_sum, (8, COLS))
+    for k in (1, 2, 3):
+        send("Gy%d" % k, gs, gy.at[k - 1], y_dev[k])
+    relay(3)
+    weight_part(0)
+    weight_part(1)
+    settle(3)
+    for k in (1, 2, 3):
+        arrive("Gy%d" % k, gy.at[k - 1])
+    gs2[...] = gs[...] + gy[0] + gy[1] + gy[2]
+    for k in (1, 2, 3):
+        send("Gl%d" % k, gs2, gl.at[k - 1], l_dev[k])
+    weight_part(2)
+    weight_part(3)
+    share = share_ref[...]
     for k in (1, 2, 3):
         arrive("L%d" % k, rl.at[k - 1])
         share = share + rl[k - 1].astype(jnp.float32)
     lat_ref[...] = share.astype(jnp.bfloat16)
-    part = jnp.sum(share * normed, axis=0, keepdims=True)
-    gs[...] = jnp.broadcast_to(part, (8, COLS))
-    for k in (1, 2, 3):
-        send("Gy%d" % k, gs, gy.at[k - 1], y_dev[k])
-    for k in (1, 2, 3):
-        arrive("Gy%d" % k, gy.at[k - 1])
-    gs2[...] = gs[...] + gy[0] + gy[1] + gy[2]
-    for k in (1, 2, 3):
-        send("Gl%d" % k, gs2, gl.at[k - 1], l_dev[k])
     for k in (1, 2, 3):
         arrive("Gl%d" % k, gl.at[k - 1])
-    gain_ref[...] = (gs2[...] + gl[0] + gl[1] + gl[2]) / GROUPS
+    gain_ref[...] = ((gs2[...] + gl[0] + gl[1] + gl[2]) / GROUPS)[0:1]
+    for k, made in level_sends:
+        @pl.when(k != 0)
+        def _(made=made):
+            made.wait_send()
     for made in started:
         made.wait_send()
 
@@ -298,7 +350,7 @@
         out_shape=(
             jax.ShapeDtypeStruct((COLS, KVC), f32),
             jax.ShapeDtypeStruct((SHARE, COLS), bf16),
-            jax.ShapeDtypeStruct((8, COLS), f32),
+            jax.ShapeDtypeStruct((1, COLS), f32),
         ),
         in_specs=[vmem] * 4,
         out_specs=(vmem,) * 3,
@@ -318,12 +370,13 @@
             pltpu.VMEM((512, COLS), bf16),
             pltpu.VMEM((512, COLS), bf16),
             pltpu.VMEM((512, COLS), bf16),
-            pltpu.VMEM((3, SHARE, COLS), bf16),
+            pltpu.VMEM((4, SHARE, COLS), bf16),
             pltpu.VMEM((3, SHARE, COLS), bf16),
             pltpu.VMEM((8, COLS), f32),
             pltpu.VMEM((3, 8, COLS), f32),
             pltpu.VMEM((8, COLS), f32),
             pltpu.VMEM((3, 8, COLS), f32),
+            pltpu.VMEM((SHARE, COLS), f32),
             pltpu.SemaphoreType.DMA((count,)),
             pltpu.SemaphoreType.DMA((count,)),
         ],
@@ -338,7 +391,7 @@
     kv_grads = attention_grads(queries[0], out_grad[0], keys[0], values[0], lengths[0])
     gain = jnp.broadcast_to(norm_gain[:, None], (COLS, 128))
     weight_grad, latent_grad, gain_grad = exchange(kv_grads, kv_weight[0], stream, gain)
-    return (weight_grad[None], latent_grad, gain_grad[0])
+    return (weight_grad[None], latent_grad, gain_grad.reshape(COLS))
 
 
 def solution(mesh):

time: 88 us -> 76 us (0.86)
  the two profiles are of different devices: /device:TPU:64 before, /device:TPU:2 now
where the time goes in v2:
time: 76 us; the launch traced here: 75.7 us
  Pallas kernels  63.2 us (83%)
  local copies, waits for them, and re-layouts  5.73 us (8%)
  matrix products  4.16 us (5%)
  between operations  1.42 us (2%)
  other arithmetic  1.19 us (2%)
    pallas_call x1, Pallas kernels, exchange(): pl.pallas_call(exchange_kernel, out_shape=(jax.ShapeDtypeStruct((COLS, KV...  63.2 us
    unnamed x17, local copies, waits for them, and re-layouts  5.58 us
    dot_general x1, matrix products, attention_grads(): jnp.einsum('gqjt,tgqd->jgd', dscore, query_h, preferred_element_type=jnp....  2.38 us

profile of v2, /device:TPU:2, one launch (start us, length us, event | category | flops | bytes accessed | tf_op | source)
XLA Modules:
  0.0 75.7 jit_solution(2225164166512652225)
XLA Ops:
  0.6 0.0 copy-start.2
  0.6 1.5 %copy.29 = bf16[16,8,32,128]{3,2,1,0:T(8,128)(2,1)S(1)} copy(bf16[16,8,32,128]{3,1,2,0:T(8,128)(2,1)} %bitcast.50) | data formatting | bytes 2097152
  2.8 0.0 copy-done.2
  2.9 0.0 copy-start.3
  2.9 0.2 copy.28
  3.1 0.6 copy-done.3
  3.7 0.5 fusion.7
  4.2 1.2 %fusion.27 = (f32[4,8,128]{2,1,0:T(8,128)S(1)}, f32[4,8,64,128]{3,2,1,0:T(8,128)}) fusion(f32[4,8,64,128]{3,2,1,0:T(8,128)S(1)} %fusion.7), kind=kOutput, calls=%fused_computation.36 | output fusion | flops 524351 | bytes 2113536 | tf_op jit(solution)/shard_map/sub | solution.py:35
  5.4 0.0 copy-start.4
  5.4 0.7 fusion.13
  6.1 0.1 copy-done.4
  6.3 0.6 convolution_bitcast_fusion
  6.9 0.0 copy-start
  6.9 2.4 %fusion.14 = bf16[4,8,8,128]{3,2,1,0:T(8,128)(2,1)S(1)} fusion(f32[4,8,64,128]{3,2,1,0:T(8,128)S(1)} %convolution_bitcast_fusion, bf16[128,4,8,128]{3,2,1,0:T(8,128)(2,1)S(1)} %bitcast.49, f32[4,8,64,128]{3,2,1,0:T(8,128)} %get-tuple-element.10, f32[4,8,128]{2,1,0:T(8,128)S(1)} %get-tuple-element.9), kind=kOutput, calls=%fused_computation.17 | convolution fusion | flops 68980800 | bytes 3227648 | tf_op jit(solution)/shard_map/gqjt,tgqd->jgd/dot_general | solution.py:41
  9.3 0.0 copy-start.1
  9.3 0.0 copy-start.5
  9.3 0.7 copy-done.5
  10.0 0.1 broadcast_in_dim.26.gn_ref
  10.1 0.0 copy-done
  10.1 0.2 copy-done.1
  10.3 63.2 %exchange.1 = (f32[256,1024]{1,0:T(8,128)S(1)}, bf16[128,256]{1,0:T(8,128)(2,1)S(1)}, f32[1,256]{1,0:T(1,128)S(1)}) custom-call(bf16[64,1024]{1,0:T(8,128)(2,1)S(1)} %pad_maximum_fusion.kv_ref, bf16[256,1024]{1,0:T(8,128)(2,1)S(1)} %bitcast.46, bf16[2048,256]{1,0:T(8,128)(2,1)S(1)} %copy-done, f32[256,128]{1,0:T(8,128)S(1)} %broadcast_in_dim.26.gn_ref), custom_call_target="tpu_custom_call" | custom-call | tf_op jit(solution)/shard_map/exchange/pallas_call | solution.py:348
  73.6 1.0 %copy.47 = f32[1,256,1024]{2,1,0:T(8,128)} copy(f32[1,256,1024]{2,1,0:T(8,128)S(1)} %bitcast.45) | data formatting | bytes 2097152
  74.5 0.6 copy.48
  75.2 0.6 copy.49
  (5 shorter events, 0.1 us)
Async XLA Ops:
  0.6 2.2 %copy-start.2 = (bf16[1,128,4096]{2,1,0:T(8,128)(2,1)S(1)}, bf16[1,128,4096]{2,1,0:T(8,128)(2,1)}, u32[]{:S(2)}) copy-start(bf16[1,128,4096]{2,1,0:T(8,128)(2,1)} %param.8) | copy-start | bytes 3145732
  2.9 0.8 %copy-start.3 = (bf16[1,64,512]{2,1,0:T(8,128)(2,1)S(1)}, bf16[1,64,512]{2,1,0:T(8,128)(2,1)}, u32[]{:S(2)}) copy-start(bf16[1,64,512]{2,1,0:T(8,128)(2,1)} %param.10) | copy-start | bytes 196612
  5.4 0.8 %copy-start.4 = (bf16[1,64,512]{2,1,0:T(8,128)(2,1)S(1)}, bf16[1,64,512]{2,1,0:T(8,128)(2,1)}, u32[]{:S(2)}) copy-start(bf16[1,64,512]{2,1,0:T(8,128)(2,1)} %param.11) | copy-start | bytes 196612
  6.9 3.3 %copy-start = (bf16[2048,256]{1,0:T(8,128)(2,1)S(1)}, bf16[2048,256]{1,0:T(8,128)(2,1)}, u32[]{:S(2)}) copy-start(bf16[2048,256]{1,0:T(8,128)(2,1)} %st_ref.1) | copy-start | bytes 3145732
  9.3 1.1 %copy-start.1 = (bf16[1,256,1024]{2,1,0:T(8,128)(2,1)S(1)}, bf16[1,256,1024]{2,1,0:T(8,128)(2,1)}, u32[]{:S(2)}) copy-start(bf16[1,256,1024]{2,1,0:T(8,128)(2,1)} %param.12) | copy-start | bytes 1572868
  9.3 0.7 copy-start.5

commit v3 on v2

--- a/solution.py
+++ b/solution.py
@@ -14,37 +14,6 @@
 
 
 NORM_EPS = 1e-05
-
-
-def attention_grads(query_rows, grad_rows, key_rows, value_rows, length):
-    token_count = query_rows.shape[0]
-    latent_count = key_rows.shape[0]
-    group_size = HQ // KVH
-    score_scale = 1.0 / math.sqrt(HD)
-    token_live = lax.iota(jnp.int32, token_count) < length
-    masked = jnp.where(token_live[:, None], grad_rows, jnp.zeros_like(grad_rows))
-    query_h = query_rows.reshape(token_count, KVH, group_size, HD)
-    grad_h = masked.reshape(token_count, KVH, group_size, HD)
-    key_h = key_rows.reshape(latent_count, KVH, HD)
-    value_h = value_rows.reshape(latent_count, KVH, HD)
-    scores = (
-        jnp.einsum("tgqd,jgd->gqjt", query_h, key_h, preferred_element_type=jnp.float32)
-        * score_scale
-    )
-    row_max = jnp.max(scores, axis=2, keepdims=True)
-    expo = jnp.exp(scores - row_max)
-    prob_values = expo / jnp.sum(expo, axis=2, keepdims=True)
-    dprob = jnp.einsum("tgqd,jgd->gqjt", grad_h, value_h, preferred_element_type=jnp.float32)
-    centre = jnp.sum(prob_values * dprob, axis=2, keepdims=True)
-    dscore = (prob_values * (dprob - centre) * score_scale).astype(jnp.bfloat16)
-    probs_b = prob_values.astype(jnp.bfloat16)
-    key_grad = jnp.einsum("gqjt,tgqd->jgd", dscore, query_h, preferred_element_type=jnp.float32)
-    value_grad = jnp.einsum("gqjt,tgqd->jgd", probs_b, grad_h, preferred_element_type=jnp.float32)
-    joined = jnp.concatenate(
-        [key_grad.reshape(latent_count, KVH * HD), value_grad.reshape(latent_count, KVH * HD)],
-        axis=1,
-    )
-    return joined.astype(jnp.bfloat16)
 
 
 ROWS = 2048
@@ -55,6 +24,8 @@
 PIPE = 16
 GROUPS = 32
 SHARE = 128
+TXT = 128
+GQ = HQ // KVH
 
 GATHER = ["Zp0", "Zm1", "Zp1", "Zm0", "Fp0", "Fm1"]
 GATHER += [n + str(i) for i in range(4) for n in ("Xp0", "Xm1", "Xp1", "Xm0", "Gp0", "Gm1")]
@@ -66,8 +37,8 @@
 
 
 def exchange_kernel(
-    kv_ref, w_ref, st_ref, gn_ref, wg_ref, lat_ref, gain_ref,
-    g, xt, latt, sq, sqz, sqx, sqc, sqs, inv, tf, tb, ro, rp, rm, sr, sl, rl, gs, gy, gs2, gl, share_ref,
+    len_ref, q_hbm, og_hbm, k_hbm, v_hbm, w_hbm, st_hbm, gn_ref, wg_ref, lat_ref, gain_ref,
+    q_ref, og_ref, k_ref, v_ref, w_ref, st_ref, kv_ref, gn_col, load_sem, g, xt, latt, sq, sqz, sqx, sqc, sqs, inv, tf, tb, ro, rp, rm, sr, sl, rl, gs, gy, gs2, gl, share_ref,
     send_sem, recv_sem,
 ):
     p = lax.axis_index("pipe")
@@ -95,6 +66,12 @@
     for peer in peers:
         pl.semaphore_signal(barrier, inc=1, device_id=peer, device_id_type=pl.DeviceIdType.MESH)
 
+    loads = []
+    pairs = ((q_hbm, q_ref), (k_hbm, k_ref), (og_hbm, og_ref), (v_hbm, v_ref), (st_hbm, st_ref), (w_hbm, w_ref))
+    for n, (src, dst) in enumerate(pairs):
+        load = pltpu.make_async_copy(src, dst, load_sem.at[n])
+        load.start()
+        loads.append(load)
     started = []
 
     def copy(name, src, dst, dev):
@@ -134,6 +111,28 @@
         sq[pl.ds(i, 1), :] = jnp.sum(turned * turned, axis=0, keepdims=True)
         return carry
 
+    token_live = lax.broadcasted_iota(jnp.int32, (1, TXT * GQ), 1) % TXT < len_ref[0]
+    for load in loads[:4]:
+        load.wait()
+    score_scale = 1.0 / math.sqrt(HD)
+    nt = (((1,), (1,)), ((), ()))
+    for kh in range(KVH):
+        cols = slice(kh * HD, (kh + 1) * HD)
+        heads = [slice((kh * GQ + i) * HD, (kh * GQ + i + 1) * HD) for i in range(GQ)]
+        query = jnp.concatenate([q_ref[:, h] for h in heads], axis=0)
+        grad = jnp.concatenate([og_ref[:, h] for h in heads], axis=0)
+        scores = lax.dot_general(k_ref[:, cols], query, nt, preferred_element_type=jnp.float32) * score_scale
+        dprob = lax.dot_general(v_ref[:, cols], grad, nt, preferred_element_type=jnp.float32)
+        dprob = jnp.where(token_live, dprob, 0.0)
+        expo = jnp.exp(scores - jnp.max(scores, axis=0, keepdims=True))
+        probs = expo * (1.0 / jnp.sum(expo, axis=0, keepdims=True))
+        centre = jnp.sum(probs * dprob, axis=0, keepdims=True)
+        dscore = (probs * (dprob - centre) * score_scale).astype(jnp.bfloat16)
+        live_probs = jnp.where(token_live, probs, 0.0).astype(jnp.bfloat16)
+        key_grad = jnp.dot(dscore, query, preferred_element_type=jnp.float32)
+        value_grad = jnp.dot(live_probs, grad, preferred_element_type=jnp.float32)
+        kv_ref[:, cols] = key_grad.astype(jnp.bfloat16)
+        kv_ref[:, kh * HD + KVH * HD : (kh + 1) * HD + KVH * HD] = value_grad.astype(jnp.bfloat16)
     pl.semaphore_wait(barrier, len(peers))
 
     for name, half, dev in (("Zp0", 0, 1), ("Zm1", 1, 3), ("Zp1", 1, 1), ("Zm0", 0, 3)):
@@ -142,9 +141,14 @@
         send(name, own(half), block(0, 0, half), x_dev[dev])
     send("C00", kv_ref, block(0, 0, None), c_dev)
     g[rows_of(zh, x, c, None), :] = kv_ref[...]
+    loads[4].wait()
     lax.fori_loop(0, ROWS // 128, squares, 0)
     for k in (1, 2, 3):
-        send("Qz%d" % k, sq, sqz.at[k - 1], z_dev[k])
+        send("Qx%d" % k, sq, sqx.at[k - 1], x_dev[k])
+    for half in range(2):
+        turned = jnp.broadcast_to(gn_ref[:, half * 128 : (half + 1) * 128], (128, 128)).T
+        gn_col[half * 128 : (half + 1) * 128, :] = turned
+    loads[5].wait()
 
     def x_send(zi, half):
         b = block(zi, 0, half)
@@ -258,37 +262,36 @@
     def normalise(i, carry):
         rows = pl.ds(pl.multiple_of(i * 128, 128), 128)
         normed = xt[:, rows].astype(jnp.float32) * inv[pl.ds(i, 1), :]
-        latt[:, rows] = (normed * gn_ref[...]).astype(jnp.bfloat16)
+        latt[:, rows] = (normed * gn_col[...]).astype(jnp.bfloat16)
         return carry
 
     x_near(0)
     x_far(0)
+    for k in (1, 2, 3):
+        arrive("Qx%d" % k, sqx.at[k - 1])
+    sqs[0] = sq[...] + sqx[0] + sqx[1] + sqx[2]
+    send("Qc", sqs.at[0], sqc, c_dev)
     terms(0)
-    relay(0)
+    arrive("Qc", sqc)
+    sqs[1] = sqs[0] + sqc[...]
+    for k in (1, 2, 3):
+        send("Qz%d" % k, sqs.at[1], sqz.at[k - 1], z_dev[k])
     arrive("Zp0", block(1, 0, 0))
     send("Fp0", block(1, 0, 0), block(1, 0, 0), z_dev[1])
     x_send(1, 0)
     arrive("Zm1", block(2, 0, 1))
     send("Fm1", block(2, 0, 1), block(2, 0, 1), z_dev[3])
     x_send(2, 1)
+    relay(0)
     arrive("Zp1", block(1, 0, 1))
     x_send(1, 1)
     core_send(1, 0)
     arrive("Zm0", block(2, 0, 0))
     x_send(2, 0)
     core_send(2, 0)
-    for k in (1, 2, 3):
-        arrive("Qz%d" % k, sqz.at[k - 1])
-    sqs[0] = sq[...] + sqz[0] + sqz[1] + sqz[2]
-    for k in (1, 2, 3):
-        send("Qx%d" % k, sqs.at[0], sqx.at[k - 1], x_dev[k])
     settle(0)
     x_near(1)
     x_near(2)
-    for k in (1, 2, 3):
-        arrive("Qx%d" % k, sqx.at[k - 1])
-    sqs[1] = sqs[0] + sqx[0] + sqx[1] + sqx[2]
-    send("Qc", sqs.at[1], sqc, c_dev)
     arrive("Fp0", block(3, 0, 0))
     x_send(3, 0)
     arrive("Fm1", block(3, 0, 1))
@@ -298,24 +301,25 @@
     x_far(2)
     terms(1)
     terms(2)
-    arrive("Qc", sqc)
-    inv[...] = lax.rsqrt((sqs[1] + sqc[...]) / D + NORM_EPS)
+    for k in (1, 2, 3):
+        arrive("Qz%d" % k, sqz.at[k - 1])
+    inv[...] = lax.rsqrt((sqs[1] + sqz[0] + sqz[1] + sqz[2]) / D + NORM_EPS)
     x_near(3)
     relay(1)
     relay(2)
     lax.fori_loop(0, ROWS // 128, normalise, 0)
-    x_far(3)
+    part_sum = gain_part(0, jnp.zeros((1, COLS), jnp.float32))
+    weight_part(0)
     settle(1)
     settle(2)
+    x_far(3)
     terms(3)
-    part_sum = jnp.zeros((1, COLS), jnp.float32)
-    for zi in range(4):
+    for zi in (1, 2, 3):
         part_sum = gain_part(zi, part_sum)
     gs[...] = jnp.broadcast_to(part_sum, (8, COLS))
     for k in (1, 2, 3):
         send("Gy%d" % k, gs, gy.at[k - 1], y_dev[k])
     relay(3)
-    weight_part(0)
     weight_part(1)
     settle(3)
     for k in (1, 2, 3):
@@ -341,7 +345,7 @@
         made.wait_send()
 
 
-def exchange(kv_grads, weight, stream, gain):
+def exchange(lengths, queries, out_grad, keys, values, weight, stream, gain):
     f32, bf16 = jnp.float32, jnp.bfloat16
     vmem = pl.BlockSpec(memory_space=pltpu.VMEM)
     count = len(SLOT)
@@ -352,9 +356,18 @@
             jax.ShapeDtypeStruct((SHARE, COLS), bf16),
             jax.ShapeDtypeStruct((1, COLS), f32),
         ),
-        in_specs=[vmem] * 4,
+        in_specs=[pl.BlockSpec(memory_space=pltpu.SMEM)] + [pl.BlockSpec(memory_space=pltpu.HBM)] * 6 + [vmem],
         out_specs=(vmem,) * 3,
         scratch_shapes=[
+            pltpu.VMEM((TXT, HQ * HD), bf16),
+            pltpu.VMEM((TXT, HQ * HD), bf16),
+            pltpu.VMEM((LAT, KVH * HD), bf16),
+            pltpu.VMEM((LAT, KVH * HD), bf16),
+            pltpu.VMEM((COLS, KVC), bf16),
+            pltpu.VMEM((ROWS, COLS), bf16),
+            pltpu.VMEM((LAT, KVC), bf16),
+            pltpu.VMEM((COLS, 128), f32),
+            pltpu.SemaphoreType.DMA((6,)),
             pltpu.VMEM((ROWS, KVC), bf16),
             pltpu.VMEM((COLS, ROWS), bf16),
             pltpu.VMEM((COLS, ROWS), bf16),
@@ -381,16 +394,16 @@
             pltpu.SemaphoreType.DMA((count,)),
         ],
         compiler_params=pltpu.CompilerParams(
-            collective_id=0, has_side_effects=True, vmem_limit_bytes=48 * 1024 * 1024
+            collective_id=0, has_side_effects=True, vmem_limit_bytes=56 * 1024 * 1024
         ),
         name="exchange",
-    )(kv_grads, weight, stream, gain)
+    )(lengths, queries, out_grad, keys, values, weight, stream, gain)
 
 
 def body(queries, out_grad, keys, values, kv_weight, stream, norm_gain, lengths):
-    kv_grads = attention_grads(queries[0], out_grad[0], keys[0], values[0], lengths[0])
-    gain = jnp.broadcast_to(norm_gain[:, None], (COLS, 128))
-    weight_grad, latent_grad, gain_grad = exchange(kv_grads, kv_weight[0], stream, gain)
+    weight_grad, latent_grad, gain_grad = exchange(
+        lengths, queries[0], out_grad[0], keys[0], values[0], kv_weight[0], stream, norm_gain.reshape(1, COLS)
+    )
     return (weight_grad[None], latent_grad, gain_grad.reshape(COLS))
 
 

time: 76 us -> 71.3 us (0.938)
  the two profiles are of different devices: /device:TPU:2 before, /device:TPU:8 now
where the time goes in v3:
time: 71.3 us; the launch traced here: 71.1 us
  Pallas kernels  66.2 us (93%)
  local copies, waits for them, and re-layouts  3.57 us (5%)
  between operations  1.3 us (2%)
    pallas_call x1, Pallas kernels, exchange(): pl.pallas_call(exchange_kernel, out_shape=(jax.ShapeDtypeStruct((COLS, KV...  66.2 us
    unnamed x7, local copies, waits for them, and re-layouts  3.57 us

profile of v3, /device:TPU:8, one launch (start us, length us, event | category | flops | bytes accessed | tf_op | source)
XLA Modules:
  0.0 71.1 jit_solution(14954616457309984809)
XLA Ops:
  1.3 66.2 %exchange.1 = (f32[256,1024]{1,0:T(8,128)}, bf16[128,256]{1,0:T(8,128)(2,1)}, f32[1,256]{1,0:T(1,128)}) custom-call(s32[1]{0:T(128)S(6)} %copy.14.len_ref, bf16[128,4096]{1,0:T(8,128)(2,1)} %bitcast.8, bf16[128,4096]{1,0:T(8,128)(2,1)} %bitcast.9, bf16[64,512]{1,0:T(8,128)(2,1)} %bitcast.12, bf16[64,512]{1,0:T(8,128)(2,1)} %bitcast.13, ...), custom_call_target="tpu_custom_call" | custom-call | tf_op jit(solution)/shard_map/exchange/pallas_call | solution.py:352
  67.5 0.0 copy-start
  67.5 2.3 %copy.15 = f32[1,256,1024]{2,1,0:T(8,128)} copy(f32[1,256,1024]{2,1,0:T(8,128)} %bitcast.10) | data formatting | bytes 2097152
  69.9 0.0 copy-done
  69.9 0.0 copy-start.1
  69.9 0.6 copy.16
  70.5 0.0 copy-done.1
  70.5 0.6 copy.17
Async XLA Ops:
  67.5 2.4 %copy-start = (bf16[128,256]{1,0:T(8,128)(2,1)S(1)}, bf16[128,256]{1,0:T(8,128)(2,1)}, u32[]{:S(2)}) copy-start(bf16[128,256]{1,0:T(8,128)(2,1)} %get-tuple-element.13) | copy-start | bytes 196612
  69.9 0.7 copy-start.1

commit v4 on v3

--- a/solution.py
+++ b/solution.py
@@ -27,8 +27,8 @@
 TXT = 128
 GQ = HQ // KVH
 
-GATHER = ["Zp0", "Zm1", "Zp1", "Zm0", "Fp0", "Fm1"]
-GATHER += [n + str(i) for i in range(4) for n in ("Xp0", "Xm1", "Xp1", "Xm0", "Gp0", "Gm1")]
+GATHER = ["Zp0", "Zm1", "Zp1", "Zm0", "Fp0a", "Fm1a", "Fp0b", "Fm1b"]
+GATHER += [n + str(i) for i in ("0", "1", "2", "3a", "3b") for n in ("Xp0", "Xm1", "Xp1", "Xm0", "Gp0", "Gm1")]
 GATHER += ["C%d%d" % (i, j) for i in range(4) for j in range(4)]
 OTHERS = ["Qz1", "Qz2", "Qz3", "Qx1", "Qx2", "Qx3", "Qc"]
 OTHERS += [n + str(h) + str(i) for i in range(4) for h in range(2) for n in ("Yo", "Yn", "Yr")]
@@ -55,10 +55,10 @@
     def pipe_dev(zz, yy):
         return (zz * 4 + yy, q)
 
-    z_dev = {k: dp_dev(up(zh, k), x, c) for k in (1, 2, 3)}
-    x_dev = {k: dp_dev(zh, up(x, k), c) for k in (1, 2, 3)}
+    z_dev = {k: dp_dev(up(zh, k), x, c) for k in (1, 3)}
+    x_dev = {k: dp_dev(zh, up(x, k), c) for k in (1, 3)}
     c_dev = dp_dev(zh, x, 1 - c)
-    y_dev = {k: pipe_dev(zl, up(y, k)) for k in (1, 2, 3)}
+    y_dev = {k: pipe_dev(zl, up(y, k)) for k in (1, 3)}
     l_dev = {k: pipe_dev(up(zl, k), y) for k in (1, 2, 3)}
     peers = [*z_dev.values(), *x_dev.values(), c_dev, *y_dev.values(), *l_dev.values()]
 
@@ -89,8 +89,21 @@
     def arrive(name, dst):
         copy(name, dst, dst, c_dev).wait_recv()
 
-    def rows_of(zz, xx, cc, half):
+    def ring_send(name, src, into, devs):
+        send(name + "1", src, into.at[0], devs[1])
+        send(name + "3", src, into.at[2], devs[3])
+
+    def ring_sum(name, src, into, devs):
+        arrive(name + "1", into.at[0])
+        send(name + "2", into.at[0], into.at[1], devs[1])
+        arrive(name + "3", into.at[2])
+        arrive(name + "2", into.at[1])
+        return src[...] + into[0] + into[1] + into[2]
+
+    def rows_of(zz, xx, cc, half, sub=None):
         start = ((zz * 4 + xx) * 2 + cc) * LAT
+        if sub is not None:
+            return pl.ds(pl.multiple_of(start + half * HALF + "ab".index(sub) * 16, 16), 16)
         if half is None:
             return pl.ds(pl.multiple_of(start, LAT), LAT)
         return pl.ds(pl.multiple_of(start + half * HALF, HALF), HALF)
@@ -98,8 +111,8 @@
     zs = [zh, up(zh, -1), up(zh, 1), up(zh, 2)]
     xs = [x, up(x, -1), up(x, 1), up(x, 2)]
 
-    def block(zi, xi, half):
-        return g.at[rows_of(zs[zi], xs[xi], c, half)]
+    def block(zi, xi, half, sub=None):
+        return g.at[rows_of(zs[zi], xs[xi], c, half, sub)]
 
     def own(half):
         return kv_ref.at[pl.ds(half * HALF, HALF)]
@@ -143,36 +156,42 @@
     g[rows_of(zh, x, c, None), :] = kv_ref[...]
     loads[4].wait()
     lax.fori_loop(0, ROWS // 128, squares, 0)
-    for k in (1, 2, 3):
-        send("Qx%d" % k, sq, sqx.at[k - 1], x_dev[k])
+    ring_send("Qx", sq, sqx, x_dev)
     for half in range(2):
         turned = jnp.broadcast_to(gn_ref[:, half * 128 : (half + 1) * 128], (128, 128)).T
         gn_col[half * 128 : (half + 1) * 128, :] = turned
     loads[5].wait()
 
-    def x_send(zi, half):
-        b = block(zi, 0, half)
-        send("Xp%d%d" % (half, zi), b, b, x_dev[1])
-        send("Xm%d%d" % (half, zi), b, b, x_dev[3])
+    def x_send(zi, half, sub=None):
+        b = block(zi, 0, half, sub)
+        tail = "%d%s" % (zi, sub or "")
+        send("Xp%d%s" % (half, tail), b, b, x_dev[1])
+        send("Xm%d%s" % (half, tail), b, b, x_dev[3])
 
     def core_send(zi, xi):
         b = block(zi, xi, None)
         send("C%d%d" % (zi, xi), b, b, c_dev)
 
-    def x_near(zi):
-        arrive("Xp0%d" % zi, block(zi, 1, 0))
-        send("Gp0%d" % zi, block(zi, 1, 0), block(zi, 1, 0), x_dev[1])
-        arrive("Xm1%d" % zi, block(zi, 2, 1))
-        send("Gm1%d" % zi, block(zi, 2, 1), block(zi, 2, 1), x_dev[3])
-        arrive("Xp1%d" % zi, block(zi, 1, 1))
-        core_send(zi, 1)
-        arrive("Xm0%d" % zi, block(zi, 2, 0))
-        core_send(zi, 2)
-
-    def x_far(zi):
-        arrive("Gp0%d" % zi, block(zi, 3, 0))
-        arrive("Gm1%d" % zi, block(zi, 3, 1))
-        core_send(zi, 3)
+    def x_near(zi, sub=None):
+        tail = "%d%s" % (zi, sub or "")
+        first, second = block(zi, 1, 0, sub), block(zi, 2, 1, sub)
+        arrive("Xp0" + tail, first)
+        send("Gp0" + tail, first, first, x_dev[1])
+        arrive("Xm1" + tail, second)
+        send("Gm1" + tail, second, second, x_dev[3])
+        arrive("Xp1" + tail, block(zi, 1, 1, sub))
+        if sub != "a":
+            core_send(zi, 1)
+        arrive("Xm0" + tail, block(zi, 2, 0, sub))
+        if sub != "a":
+            core_send(zi, 2)
+
+    def x_far(zi, sub=None):
+        tail = "%d%s" % (zi, sub or "")
+        arrive("Gp0" + tail, block(zi, 3, 0, sub))
+        arrive("Gm1" + tail, block(zi, 3, 1, sub))
+        if sub != "a":
+            core_send(zi, 3)
 
     yo, yp, ym = up(y, 2), up(y, 1), up(y, -1)
 
@@ -265,22 +284,27 @@
         latt[:, rows] = (normed * gn_col[...]).astype(jnp.bfloat16)
         return carry
 
+    def far_z(sub):
+        arrive("Fp0" + sub, block(3, 0, 0, sub))
+        x_send(3, 0, sub)
+        arrive("Fm1" + sub, block(3, 0, 1, sub))
+        x_send(3, 1, sub)
+
     x_near(0)
     x_far(0)
-    for k in (1, 2, 3):
-        arrive("Qx%d" % k, sqx.at[k - 1])
-    sqs[0] = sq[...] + sqx[0] + sqx[1] + sqx[2]
+    sqs[0] = ring_sum("Qx", sq, sqx, x_dev)
     send("Qc", sqs.at[0], sqc, c_dev)
     terms(0)
     arrive("Qc", sqc)
     sqs[1] = sqs[0] + sqc[...]
-    for k in (1, 2, 3):
-        send("Qz%d" % k, sqs.at[1], sqz.at[k - 1], z_dev[k])
+    ring_send("Qz", sqs.at[1], sqz, z_dev)
     arrive("Zp0", block(1, 0, 0))
-    send("Fp0", block(1, 0, 0), block(1, 0, 0), z_dev[1])
+    for sub in "ab":
+        send("Fp0" + sub, block(1, 0, 0, sub), block(1, 0, 0, sub), z_dev[1])
     x_send(1, 0)
     arrive("Zm1", block(2, 0, 1))
-    send("Fm1", block(2, 0, 1), block(2, 0, 1), z_dev[3])
+    for sub in "ab":
+        send("Fm1" + sub, block(2, 0, 1, sub), block(2, 0, 1, sub), z_dev[3])
     x_send(2, 1)
     relay(0)
     arrive("Zp1", block(1, 0, 1))
@@ -292,41 +316,38 @@
     settle(0)
     x_near(1)
     x_near(2)
-    arrive("Fp0", block(3, 0, 0))
-    x_send(3, 0)
-    arrive("Fm1", block(3, 0, 1))
-    x_send(3, 1)
+    far_z("a")
+    x_far(1)
+    far_z("b")
     core_send(3, 0)
-    x_far(1)
+    x_near(3, "a")
     x_far(2)
     terms(1)
+    x_near(3, "b")
     terms(2)
-    for k in (1, 2, 3):
-        arrive("Qz%d" % k, sqz.at[k - 1])
-    inv[...] = lax.rsqrt((sqs[1] + sqz[0] + sqz[1] + sqz[2]) / D + NORM_EPS)
-    x_near(3)
+    total_squares = ring_sum("Qz", sqs.at[1], sqz, z_dev)
+    inv[...] = lax.rsqrt(total_squares / D + NORM_EPS)
     relay(1)
+    x_far(3, "a")
     relay(2)
+    part_sum = jnp.zeros((1, COLS), jnp.float32)
+    for zi in range(3):
+        part_sum = gain_part(zi, part_sum)
+    x_far(3, "b")
     lax.fori_loop(0, ROWS // 128, normalise, 0)
-    part_sum = gain_part(0, jnp.zeros((1, COLS), jnp.float32))
+    settle(1)
+    terms(3)
+    part_sum = gain_part(3, part_sum)
+    gs[...] = jnp.broadcast_to(part_sum, (8, COLS))
+    ring_send("Gy", gs, gy, y_dev)
+    settle(2)
     weight_part(0)
-    settle(1)
-    settle(2)
-    x_far(3)
-    terms(3)
-    for zi in (1, 2, 3):
-        part_sum = gain_part(zi, part_sum)
-    gs[...] = jnp.broadcast_to(part_sum, (8, COLS))
-    for k in (1, 2, 3):
-        send("Gy%d" % k, gs, gy.at[k - 1], y_dev[k])
     relay(3)
     weight_part(1)
-    settle(3)
-    for k in (1, 2, 3):
-        arrive("Gy%d" % k, gy.at[k - 1])
-    gs2[...] = gs[...] + gy[0] + gy[1] + gy[2]
+    gs2[...] = ring_sum("Gy", gs, gy, y_dev)
     for k in (1, 2, 3):
         send("Gl%d" % k, gs2, gl.at[k - 1], l_dev[k])
+    settle(3)
     weight_part(2)
     weight_part(3)
     share = share_ref[...]

time: 71.3 us -> 71.1 us (level)
  the two profiles are of different devices: /device:TPU:8 before, /device:TPU:64 now
where the time goes in v4:
time: 71.1 us; the launch traced here: 70.9 us
  Pallas kernels  66 us (93%)
  local copies, waits for them, and re-layouts  3.57 us (5%)
  between operations  1.3 us (2%)
    pallas_call x1, Pallas kernels, exchange(): pl.pallas_call(exchange_kernel, out_shape=(jax.ShapeDtypeStruct((COLS, KV...  66 us
    unnamed x7, local copies, waits for them, and re-layouts  3.57 us

profile of v4, /device:TPU:64, one launch (start us, length us, event | category | flops | bytes accessed | tf_op | source)
XLA Modules:
  0.0 70.9 jit_solution(469289725864105101)
XLA Ops:
  1.3 66.0 %exchange.1 = (f32[256,1024]{1,0:T(8,128)}, bf16[128,256]{1,0:T(8,128)(2,1)}, f32[1,256]{1,0:T(1,128)}) custom-call(s32[1]{0:T(128)S(6)} %copy.14.len_ref, bf16[128,4096]{1,0:T(8,128)(2,1)} %bitcast.8, bf16[128,4096]{1,0:T(8,128)(2,1)} %bitcast.9, bf16[64,512]{1,0:T(8,128)(2,1)} %bitcast.12, bf16[64,512]{1,0:T(8,128)(2,1)} %bitcast.13, ...), custom_call_target="tpu_custom_call" | custom-call | tf_op jit(solution)/shard_map/exchange/pallas_call | solution.py:373
  67.3 0.0 copy-start
  67.3 2.3 %copy.15 = f32[1,256,1024]{2,1,0:T(8,128)} copy(f32[1,256,1024]{2,1,0:T(8,128)} %bitcast.10) | data formatting | bytes 2097152
  69.7 0.0 copy-done
  69.7 0.0 copy-start.1
  69.7 0.6 copy.16
  70.3 0.0 copy-done.1
  70.3 0.6 copy.17
Async XLA Ops:
  67.3 2.4 %copy-start = (bf16[128,256]{1,0:T(8,128)(2,1)S(1)}, bf16[128,256]{1,0:T(8,128)(2,1)}, u32[]{:S(2)}) copy-start(bf16[128,256]{1,0:T(8,128)(2,1)} %get-tuple-element.13) | copy-start | bytes 196612
  69.7 0.7 copy-start.1

commit v5 on v4

--- a/solution.py
+++ b/solution.py
@@ -58,7 +58,7 @@
     z_dev = {k: dp_dev(up(zh, k), x, c) for k in (1, 3)}
     x_dev = {k: dp_dev(zh, up(x, k), c) for k in (1, 3)}
     c_dev = dp_dev(zh, x, 1 - c)
-    y_dev = {k: pipe_dev(zl, up(y, k)) for k in (1, 3)}
+    y_dev = {k: pipe_dev(zl, up(y, k)) for k in (1, 2, 3)}
     l_dev = {k: pipe_dev(up(zl, k), y) for k in (1, 2, 3)}
     peers = [*z_dev.values(), *x_dev.values(), c_dev, *y_dev.values(), *l_dev.values()]
 
@@ -327,28 +327,31 @@
     terms(2)
     total_squares = ring_sum("Qz", sqs.at[1], sqz, z_dev)
     inv[...] = lax.rsqrt(total_squares / D + NORM_EPS)
+    lax.fori_loop(0, ROWS // 128, normalise, 0)
     relay(1)
     x_far(3, "a")
     relay(2)
+    weight_part(0)
     part_sum = jnp.zeros((1, COLS), jnp.float32)
     for zi in range(3):
         part_sum = gain_part(zi, part_sum)
     x_far(3, "b")
-    lax.fori_loop(0, ROWS // 128, normalise, 0)
     settle(1)
+    weight_part(1)
     terms(3)
     part_sum = gain_part(3, part_sum)
     gs[...] = jnp.broadcast_to(part_sum, (8, COLS))
-    ring_send("Gy", gs, gy, y_dev)
+    for k in (1, 2, 3):
+        send("Gy%d" % k, gs, gy.at[k - 1], y_dev[k])
     settle(2)
-    weight_part(0)
     relay(3)
-    weight_part(1)
-    gs2[...] = ring_sum("Gy", gs, gy, y_dev)
+    weight_part(2)
+    for k in (1, 2, 3):
+        arrive("Gy%d" % k, gy.at[k - 1])
+    gs2[...] = gs[...] + gy[0] + gy[1] + gy[2]
     for k in (1, 2, 3):
         send("Gl%d" % k, gs2, gl.at[k - 1], l_dev[k])
     settle(3)
-    weight_part(2)
     weight_part(3)
     share = share_ref[...]
     for k in (1, 2, 3):

time: 71.1 us -> 70.2 us (0.987)
  Pallas kernels: 66 us -> 65.1 us
    pallas_call x1, Pallas kernels: 66 us -> 65.1 us  [exchange(): pl.pallas_call(exchange_kernel, out_shape=(jax.ShapeDtypeStruct((COLS, KV...]
where the time goes in v5:
time: 70.2 us; the launch traced here: 70 us
  Pallas kernels  65.1 us (93%)
  local copies, waits for them, and re-layouts  3.57 us (5%)
  between operations  1.3 us (2%)
    pallas_call x1, Pallas kernels, exchange(): pl.pallas_call(exchange_kernel, out_shape=(jax.ShapeDtypeStruct((COLS, KV...  65.1 us
    unnamed x7, local copies, waits for them, and re-layouts  3.57 us

profile of v5, /device:TPU:64, one launch (start us, length us, event | category | flops | bytes accessed | tf_op | source)
XLA Modules:
  0.0 70.0 jit_solution(8917475148190453313)
XLA Ops:
  1.3 65.1 %exchange.1 = (f32[256,1024]{1,0:T(8,128)}, bf16[128,256]{1,0:T(8,128)(2,1)}, f32[1,256]{1,0:T(1,128)}) custom-call(s32[1]{0:T(128)S(6)} %copy.14.len_ref, bf16[128,4096]{1,0:T(8,128)(2,1)} %bitcast.8, bf16[128,4096]{1,0:T(8,128)(2,1)} %bitcast.9, bf16[64,512]{1,0:T(8,128)(2,1)} %bitcast.12, bf16[64,512]{1,0:T(8,128)(2,1)} %bitcast.13, ...), custom_call_target="tpu_custom_call" | custom-call | tf_op jit(solution)/shard_map/exchange/pallas_call | solution.py:376
  66.4 0.0 copy-start
  66.4 2.3 %copy.15 = f32[1,256,1024]{2,1,0:T(8,128)} copy(f32[1,256,1024]{2,1,0:T(8,128)} %bitcast.10) | data formatting | bytes 2097152
  68.8 0.0 copy-done
  68.8 0.0 copy-start.1
  68.8 0.6 copy.16
  69.4 0.0 copy-done.1
  69.4 0.6 copy.17
Async XLA Ops:
  66.4 2.4 %copy-start = (bf16[128,256]{1,0:T(8,128)(2,1)S(1)}, bf16[128,256]{1,0:T(8,128)(2,1)}, u32[]{:S(2)}) copy-start(bf16[128,256]{1,0:T(8,128)(2,1)} %get-tuple-element.13) | copy-start | bytes 196612
  68.8 0.7 copy-start.1
